TPU v7x, 32 devices: a whole 2x2x4 slice. The times are simulated.
32 devices in a mesh: fsdp: 16 (over z, y, core), dp: 2 (over x).
Axes of the slice: x: 2, y: 2, z: 4, core: 2. Of those that a mesh axis runs over, the one named last changes fastest.
Arguments:
- tokens: bfloat16 [32, 256, 1152], P(('fsdp', 'dp')), may hold values from -12 to 12, as said below
- cond: bfloat16 [32, 1152], P(('fsdp', 'dp')), may hold values from -6 to 6
- segment_ids: int32 [32, 256], P(('fsdp', 'dp')), may hold values from 0 to 7, as said below
- ada_weight: bfloat16 [1152, 6912], P('fsdp'), may hold values from -0.1875 to 0.1875
- ada_bias: bfloat16 [6912], P('fsdp'), may hold values from -1 to 1
- qkv_weight: bfloat16 [1152, 3456], P('fsdp'), may hold values from -0.1875 to 0.1875
- qv_bias: bfloat16 [2304], P('fsdp'), may hold values from -1 to 1
- proj_weight: bfloat16 [1152, 1152], P('fsdp'), may hold values from -0.75 to 0.75
- proj_bias: bfloat16 [1152], P('fsdp'), may hold values from -1 to 1
- fc1_weight: bfloat16 [1152, 4608], P('fsdp'), may hold values from -0.1875 to 0.1875
- fc1_bias: bfloat16 [4608], P('fsdp'), may hold values from -1 to 1
- fc2_weight: bfloat16 [4608, 1152], P('fsdp'), may hold values from -0.09375 to 0.09375
- fc2_bias: bfloat16 [1152], P('fsdp'), may hold values from -1 to 1
- out_grad: bfloat16 [32, 256, 1152], P(('fsdp', 'dp')), may hold values from -6 to 6
Outputs:
- output: bfloat16 [32, 256, 1152], P(('fsdp', 'dp'))
- tokens_grad: bfloat16 [32, 256, 1152], P(('fsdp', 'dp'))
- ada_weight_grad: float32 [1152, 6912], P('fsdp')
- ada_bias_grad: float32 [6912], P('fsdp')
- qkv_weight_grad: float32 [1152, 3456], P('fsdp')
- qv_bias_grad: float32 [2304], P('fsdp')
- proj_weight_grad: float32 [1152, 1152], P('fsdp')
- proj_bias_grad: float32 [1152], P('fsdp')
- fc1_weight_grad: float32 [1152, 4608], P('fsdp')
- fc1_bias_grad: float32 [4608], P('fsdp')
- fc2_weight_grad: float32 [4608, 1152], P('fsdp')
- fc2_bias_grad: float32 [1152], P('fsdp')
Inputs may be any that keep to these rules, and one draw needn't show every extreme that they name: `segment_ids`: each row holds whole images one after another, numbered from 0 in order: eight images of 32 tokens, or two of 128 tokens, or one of 128 tokens among four of 32 tokens. Some row holds eight images and some row holds two. `tokens`: token features.
All inputs are finite; a program needn't handle non-finite values.
Results may differ from a plain program's by a relative error of at most 0.02.
The roundings to bfloat16 on the way count: a program that leaves them out, or rounds other values in their place, can miss the bound.
Values may be sent and summed in bfloat16 or wider, within the bound.
A program may use at most 384 MiB of HBM per device.

v0:
```python
import jax
import jax.numpy as jnp
from jax import lax
from jax.sharding import PartitionSpec as P

HEADS = 16
HEAD_DIM = 72
root_half = 0.7978845608028654
norm_eps = 1e-06
masked_score = -1e30


def gelu_tanh(stream):
    return (
        0.5 * stream * (1.0 + jnp.tanh(root_half * (stream + 0.044715 * stream * stream * stream)))
    )


def gelu_slope(stream):
    tanh_inner = jnp.tanh(root_half * (stream + 0.044715 * stream * stream * stream))
    return 0.5 * (1.0 + tanh_inner) + 0.5 * stream * (1.0 - tanh_inner * tanh_inner) * root_half * (
        1.0 + 3.0 * 0.044715 * stream * stream
    )


def normalize(stream):
    centre = jnp.mean(stream, axis=-1, keepdims=True)
    centred = stream - centre
    inv_std = lax.rsqrt(jnp.mean(centred * centred, axis=-1, keepdims=True) + norm_eps)
    return (centred * inv_std, inv_std)


def normalize_back(incoming, normed, inv_std):
    return inv_std * (
        incoming
        - jnp.mean(incoming, axis=-1, keepdims=True)
        - normed * jnp.mean(incoming * normed, axis=-1, keepdims=True)
    )


def head_scores(projected, same_doc, head_index, model_width):
    query_part = lax.dynamic_slice_in_dim(projected, head_index * HEAD_DIM, HEAD_DIM, 1)
    key_part = lax.dynamic_slice_in_dim(projected, model_width + head_index * HEAD_DIM, HEAD_DIM, 1)
    value_part = lax.dynamic_slice_in_dim(
        projected, 2 * model_width + head_index * HEAD_DIM, HEAD_DIM, 1
    )
    raw_scores = jnp.einsum(
        "qd,kd->qk", query_part, key_part, preferred_element_type=jnp.float32
    ) * HEAD_DIM ** (-0.5)
    return (jnp.where(same_doc, raw_scores, masked_score), query_part, key_part, value_part)


def merge_heads(stacked, model_width):
    return jnp.transpose(stacked, (1, 0, 2)).reshape(stacked.shape[1], model_width)


def attend_row(projected, segments_row, model_width):
    same_doc = segments_row[:, None] == segments_row[None, :]

    def one_head(head_index):
        scores, query_part, key_part, value_part = head_scores(
            projected, same_doc, head_index, model_width
        )
        top_score = jnp.max(scores, axis=-1, keepdims=True)
        exp_scores = jnp.exp(scores - top_score)
        denominator = jnp.sum(exp_scores, axis=-1, keepdims=True)
        probabilities = (exp_scores / denominator).astype(jnp.bfloat16)
        mixed_heads = jnp.dot(probabilities, value_part, preferred_element_type=jnp.float32)
        return (mixed_heads, (top_score + jnp.log(denominator))[:, 0])

    mixed_heads, log_total = lax.map(one_head, jnp.arange(HEADS))
    return (merge_heads(mixed_heads, model_width).astype(jnp.bfloat16), log_total)


def attend_back(projected, segments_row, log_total, d_mixed, model_width):
    same_doc = segments_row[:, None] == segments_row[None, :]
    head_scale = HEAD_DIM ** (-0.5)

    def one_head(head_index):
        scores, query_part, key_part, value_part = head_scores(
            projected, same_doc, head_index, model_width
        )
        d_head = lax.dynamic_slice_in_dim(d_mixed, head_index * HEAD_DIM, HEAD_DIM, 1)
        lse_row = lax.dynamic_index_in_dim(log_total, head_index, 0, keepdims=False)
        probabilities = jnp.exp(scores - lse_row[:, None])
        prob_low = probabilities.astype(jnp.bfloat16)
        d_probs = jnp.einsum("qd,kd->qk", d_head, value_part, preferred_element_type=jnp.float32)
        d_value = jnp.einsum("qk,qd->kd", prob_low, d_head, preferred_element_type=jnp.float32)
        d_scores = (
            probabilities * (d_probs - jnp.sum(d_probs * probabilities, axis=-1, keepdims=True))
        ).astype(jnp.bfloat16)
        d_query = (
            jnp.einsum("qk,kd->qd", d_scores, key_part, preferred_element_type=jnp.float32)
            * head_scale
        )
        d_key = (
            jnp.einsum("qk,qd->kd", d_scores, query_part, preferred_element_type=jnp.float32)
            * head_scale
        )
        return (d_query, d_key, d_value)

    d_query, d_key, d_value = lax.map(one_head, jnp.arange(HEADS))
    merged = [
        merge_heads(d_query, model_width),
        merge_heads(d_key, model_width),
        merge_heads(d_value, model_width),
    ]
    return jnp.concatenate(merged, axis=-1).astype(jnp.bfloat16)


def on_device(
    tokens,
    cond,
    segment_ids,
    ada_weight,
    ada_bias,
    qkv_weight,
    qv_bias,
    proj_weight,
    proj_bias,
    fc1_weight,
    fc1_bias,
    fc2_weight,
    fc2_bias,
    out_grad,
):
    row_count, seq_len, model_width = tokens.shape
    ff_width = fc1_weight.shape[1]
    stream = tokens.astype(jnp.float32)
    cond_float = cond.astype(jnp.float32)
    cond_act = (cond_float / (1.0 + jnp.exp(-cond_float))).astype(jnp.bfloat16)
    fsdp_at, dp_at = (lax.axis_index("fsdp"), lax.axis_index("dp"))
    dp_size = lax.axis_size("dp")
    slice_width, bias_width = (ada_weight.shape[0], ada_bias.shape[0])
    act_all = lax.all_gather(cond_act, ("fsdp", "dp"), axis=0, tiled=True)
    act_mine = lax.dynamic_slice_in_dim(act_all, fsdp_at * slice_width, slice_width, 1)
    partial = jnp.dot(act_mine, ada_weight, preferred_element_type=jnp.float32)
    bias_row = lax.dynamic_update_slice_in_dim(
        jnp.zeros((6 * model_width,), jnp.float32),
        ada_bias.astype(jnp.float32),
        fsdp_at * bias_width,
        0,
    )
    partial = (partial + bias_row).reshape(-1, dp_size, row_count, 6 * model_width)
    partial = lax.dynamic_index_in_dim(partial, dp_at, 1, keepdims=False)
    modulation = lax.psum_scatter(
        partial.reshape(-1, 6 * model_width), "fsdp", scatter_dimension=0, tiled=True
    )
    pieces = [
        modulation[:, None, section * model_width : (section + 1) * model_width]
        for section in range(6)
    ]
    shift_one, scale_one, gate_one, shift_two, scale_two, gate_two = pieces
    qkv_full, qv_bias_full, proj_full, proj_bias_full = (
        lax.all_gather(qkv_weight, "fsdp", axis=0, tiled=True),
        lax.all_gather(qv_bias, "fsdp", axis=0, tiled=True),
        lax.all_gather(proj_weight, "fsdp", axis=0, tiled=True),
        lax.all_gather(proj_bias, "fsdp", axis=0, tiled=True),
    )
    normed_one, inv_one = normalize(stream)
    hidden_one = (normed_one * (1.0 + scale_one) + shift_one).astype(jnp.bfloat16)
    qv_float = qv_bias_full.astype(jnp.float32)
    qkv_bias = jnp.concatenate(
        [qv_float[:model_width], jnp.zeros((model_width,), jnp.float32), qv_float[model_width:]]
    )
    projected = (
        jnp.dot(hidden_one, qkv_full, preferred_element_type=jnp.float32) + qkv_bias
    ).astype(jnp.bfloat16)

    def row_forward(row_items):
        return attend_row(row_items[0], row_items[1], model_width)

    mixed_rows, log_total = lax.map(row_forward, (projected, segment_ids))
    branch_one = jnp.dot(
        mixed_rows, proj_full, preferred_element_type=jnp.float32
    ) + proj_bias_full.astype(jnp.float32)
    resid_one = stream + gate_one * branch_one
    fc1_full, fc1_bias_full, fc2_full, fc2_bias_full = (
        lax.all_gather(fc1_weight, "fsdp", axis=0, tiled=True),
        lax.all_gather(fc1_bias, "fsdp", axis=0, tiled=True),
        lax.all_gather(fc2_weight, "fsdp", axis=0, tiled=True),
        lax.all_gather(fc2_bias, "fsdp", axis=0, tiled=True),
    )
    normed_two, inv_two = normalize(resid_one)
    hidden_two = (normed_two * (1.0 + scale_two) + shift_two).astype(jnp.bfloat16)
    pre_act = jnp.dot(
        hidden_two, fc1_full, preferred_element_type=jnp.float32
    ) + fc1_bias_full.astype(jnp.float32)
    active = gelu_tanh(pre_act).astype(jnp.bfloat16)
    branch_two = jnp.dot(
        active, fc2_full, preferred_element_type=jnp.float32
    ) + fc2_bias_full.astype(jnp.float32)
    output = (resid_one + gate_two * branch_two).astype(jnp.bfloat16)
    d_out = out_grad.astype(jnp.float32)
    fc1_back, fc2_back = (
        lax.all_gather(fc1_weight, "fsdp", axis=0, tiled=True),
        lax.all_gather(fc2_weight, "fsdp", axis=0, tiled=True),
    )
    d_gate_two = jnp.sum(d_out * branch_two, axis=1)
    d_branch_two = (d_out * gate_two).astype(jnp.bfloat16)
    fc2_shard = lax.psum_scatter(
        jnp.einsum("rsf,rsd->fd", active, d_branch_two, preferred_element_type=jnp.float32).astype(
            jnp.bfloat16
        ),
        "fsdp",
        scatter_dimension=0,
        tiled=True,
    )
    grad_fc2_bias = jnp.sum(d_branch_two.astype(jnp.float32), axis=(0, 1))
    d_active = jnp.einsum("rsd,fd->rsf", d_branch_two, fc2_back, preferred_element_type=jnp.float32)
    d_pre = (d_active * gelu_slope(pre_act)).astype(jnp.bfloat16)
    grad_fc1_bias = jnp.sum(d_pre.astype(jnp.float32), axis=(0, 1))
    d_hidden_two = jnp.einsum("rsf,ef->rse", d_pre, fc1_back, preferred_element_type=jnp.float32)
    d_scale_two = jnp.sum(d_hidden_two * normed_two, axis=1)
    d_shift_two = jnp.sum(d_hidden_two, axis=1)
    d_resid = d_out + normalize_back(d_hidden_two * (1.0 + scale_two), normed_two, inv_two)
    qkv_back, proj_back = (
        lax.all_gather(qkv_weight, "fsdp", axis=0, tiled=True),
        lax.all_gather(proj_weight, "fsdp", axis=0, tiled=True),
    )
    d_gate_one = jnp.sum(d_resid * branch_one, axis=1)
    d_branch_one = (d_resid * gate_one).astype(jnp.bfloat16)
    grad_proj_bias = jnp.sum(d_branch_one.astype(jnp.float32), axis=(0, 1))
    d_mixed = jnp.einsum(
        "rsd,ed->rse", d_branch_one, proj_back, preferred_element_type=jnp.float32
    ).astype(jnp.bfloat16)

    def row_backward(row_items):
        return attend_back(row_items[0], row_items[1], row_items[2], row_items[3], model_width)

    d_projected = lax.map(row_backward, (projected, segment_ids, log_total, d_mixed))
    d_proj_float = d_projected.astype(jnp.float32)
    grad_qv_bias = jnp.concatenate(
        [
            jnp.sum(d_proj_float[..., :model_width], axis=(0, 1)),
            jnp.sum(d_proj_float[..., 2 * model_width :], axis=(0, 1)),
        ]
    )
    d_hidden_one = jnp.einsum(
        "rsf,ef->rse", d_projected, qkv_back, preferred_element_type=jnp.float32
    )
    d_scale_one = jnp.sum(d_hidden_one * normed_one, axis=1)
    d_shift_one = jnp.sum(d_hidden_one, axis=1)
    tokens_grad = (
        d_resid + normalize_back(d_hidden_one * (1.0 + scale_one), normed_one, inv_one)
    ).astype(jnp.bfloat16)
    d_modulation = jnp.concatenate(
        [d_shift_one, d_scale_one, d_gate_one, d_shift_two, d_scale_two, d_gate_two], axis=-1
    ).astype(jnp.bfloat16)
    d_mod_all = lax.all_gather(d_modulation, ("fsdp", "dp"), axis=0, tiled=True)
    grad_ada = jnp.einsum("rd,re->de", act_mine, d_mod_all, preferred_element_type=jnp.float32)
    grad_ada_bias = jnp.sum(
        lax.dynamic_slice_in_dim(d_mod_all, fsdp_at * bias_width, bias_width, 1).astype(
            jnp.float32
        ),
        axis=0,
    )

    def owners(term):
        return lax.psum_scatter(term.astype(jnp.bfloat16), "fsdp", scatter_dimension=0, tiled=True)

    qkv_shard = owners(
        jnp.einsum("rse,rsf->ef", hidden_one, d_projected, preferred_element_type=jnp.float32)
    )
    proj_shard = owners(
        jnp.einsum("rse,rsd->ed", mixed_rows, d_branch_one, preferred_element_type=jnp.float32)
    )
    fc1_shard = owners(
        jnp.einsum("rse,rsf->ef", hidden_two, d_pre, preferred_element_type=jnp.float32)
    )
    bias_shards = (
        None,
        lax.psum_scatter(
            grad_qv_bias.astype(jnp.bfloat16), "fsdp", scatter_dimension=0, tiled=True
        ).astype(jnp.float32),
        lax.psum_scatter(
            grad_proj_bias.astype(jnp.bfloat16), "fsdp", scatter_dimension=0, tiled=True
        ).astype(jnp.float32),
        lax.psum_scatter(
            grad_fc1_bias.astype(jnp.bfloat16), "fsdp", scatter_dimension=0, tiled=True
        ).astype(jnp.float32),
        lax.psum_scatter(
            grad_fc2_bias.astype(jnp.bfloat16), "fsdp", scatter_dimension=0, tiled=True
        ).astype(jnp.float32),
    )
    summed = (
        grad_ada,
        grad_ada_bias,
        lax.psum(qkv_shard.astype(jnp.bfloat16), "dp").astype(jnp.float32),
        lax.psum(bias_shards[1].astype(jnp.bfloat16), "dp").astype(jnp.float32),
        lax.psum(proj_shard.astype(jnp.bfloat16), "dp").astype(jnp.float32),
        lax.psum(bias_shards[2].astype(jnp.bfloat16), "dp").astype(jnp.float32),
        lax.psum(fc1_shard.astype(jnp.bfloat16), "dp").astype(jnp.float32),
        lax.psum(bias_shards[3].astype(jnp.bfloat16), "dp").astype(jnp.float32),
        lax.psum(fc2_shard, "dp").astype(jnp.float32),
        lax.psum(bias_shards[4].astype(jnp.bfloat16), "dp").astype(jnp.float32),
    )
    return (
        output,
        tokens_grad,
        summed[0],
        summed[1],
        summed[2],
        summed[3],
        summed[4],
        summed[5],
        summed[6],
        summed[7],
        summed[8],
        summed[9],
    )


def solution(mesh):
    in_specs = (
        P(("fsdp", "dp"), None, None),
        P(("fsdp", "dp"), None),
        P(("fsdp", "dp"), None),
        P("fsdp", None),
        P("fsdp"),
        P("fsdp", None),
        P("fsdp"),
        P("fsdp", None),
        P("fsdp"),
        P("fsdp", None),
        P("fsdp"),
        P("fsdp", None),
        P("fsdp"),
        P(("fsdp", "dp"), None, None),
    )
    out_specs = (
        P(("fsdp", "dp"), None, None),
        P(("fsdp", "dp"), None, None),
        P("fsdp", None),
        P("fsdp"),
        P("fsdp", None),
        P("fsdp"),
        P("fsdp", None),
        P("fsdp"),
        P("fsdp", None),
        P("fsdp"),
        P("fsdp", None),
        P("fsdp"),
    )
    return jax.shard_map(
        on_device, mesh=mesh, in_specs=in_specs, out_specs=out_specs, check_vma=False
    )
```

profile of v0, /device:TPU:0, one launch (start us, length us, event | category | flops | bytes accessed | tf_op | source)
XLA Modules:
  0.0 1116.8 jit_solution(17571524379434750017)
XLA Ops:
  8.0 70.5 %all-gather = bf16[32,1,1152]{2,1,0:T(2,128)(2,1)S(1)} all-gather(bf16[1,1,1152]{2,1,0:T(2,128)(2,1)S(1)} %convert_bitcast_fusion), channel_id=1, replica_groups=mesh['fsdp'=16,'dp'=2] {'fsdp','dp'}, dimensions={0}, use_global_device_ids=true | all-gather | bytes 76032 | tf_op jit(solution)/shard_map/all_gather | solution.py:135
  87.5 57.8 %all-reduce.12 = (bf16[2304]{0:T(1024)(128)(2,1)S(1)}, bf16[1152]{0:T(1024)(128)(2,1)S(1)}, bf16[4608]{0:T(1024)(128)(2,1)S(1)}) all-reduce(bf16[2304]{0:T(1024)(128)(2,1)S(1)} %dynamic-update-slice, bf16[1152]{0:T(1024)(128)(2,1)S(1)} %dynamic-update-slice.1, ...), channel_id=1, replica_groups=mesh['fsdp'=16,'dp'=2] {'fsdp'}, use_global_device_ids=true, to_apply=%add | all-reduce | flops 8064 | bytes 32256
  145.8 22.1 %all-reduce.18.cloned.1.call-done = f32[16,6912]{1,0:T(8,128)} async-done(((f32[16,6912]{1,0:T(8,128)}), f32[16,6912]{1,0:T(8,128)}) %all-reduce.18.cloned.1.call-update) | async-done | bytes 442384
  169.6 72.5 %all-gather.7.cloned.1.call-done = bf16[1152,3456]{1,0:T(8,128)(2,1)} async-done(((bf16[72,3456]{1,0:T(8,128)(2,1)}), bf16[1152,3456]{1,0:T(8,128)(2,1)}) %all-gather.7.cloned.1.call-update) | async-done | bytes 7962640 | tf_op jit(solution)/shard_map/all_gather | solution.py:155
  242.2 6.0 fusion.37
  248.2 32.0 %while.50 = (s32[]{:T(128)}, bf16[16,256,72]{1,2,0:T(8,128)(2,1)S(1)}, f32[16,256]{1,0:T(8,128)S(1)}, s32[16]{0:T(128)S(1)}, bf16[256,3456]{1,0:T(8,128)(2,1)S(1...) while((s32[]{:T(128)}, ...), condition=%wide.region_6.7_spmd.clone, body=%wide.region_3.6_spmd.clone.sunk | while | flops 19463948 | bytes 1069367 | solution.py:71
  280.3 6.1 all-gather.9.cloned.1.call-done
  286.4 3.9 fusion.89
  290.5 85.2 %all-gather.11.cloned.1.call-done = bf16[1152,4608]{1,0:T(8,128)(2,1)} async-done(((bf16[72,4608]{1,0:T(8,128)(2,1)}), bf16[1152,4608]{1,0:T(8,128)(2,1)}) %all-gather.11.cloned.1.call-update) | async-done | bytes 10616848 | tf_op jit(solution)/shard_map/all_gather | solution.py:179
  375.7 9.1 convolution_add_fusion.1
  384.8 79.7 %all-gather.13.cloned.1.call-done = bf16[4608,1152]{1,0:T(8,128)(2,1)} async-done(((bf16[288,1152]{1,0:T(8,128)(2,1)}), bf16[4608,1152]{1,0:T(8,128)(2,1)}) %all-gather.13.cloned.1.call-update) | async-done | bytes 10616848 | tf_op jit(solution)/shard_map/all_gather | solution.py:181
  464.5 8.5 fusion.93
  473.0 8.3 fusion.60
  484.2 2.5 convolution_convert_fusion.3
  486.8 3.8 convolution_convert_fusion.4
  493.1 179.2 %while.51 = (s32[]{:T(128)}, bf16[16,256,72]{1,2,0:T(8,128)(2,1)}, bf16[16,256,72]{1,2,0:T(8,128)(2,1)}, bf16[16,256,72]{1,2,0:T(8,128)(2,1)}, s32[16]{0:T(128)S...) while((s32[]{:T(128)}, bf16[16,256,72]{1,2,0:T(8,128)(2,1)}, ...), condition=%wide.region_13.14_spmd.clone, body=%wide.region_11.13_spmd.clone.sunk | while | flops 47877904 | bytes 2653598 | solution.py:102
  499.0 1.8 fusion.138
  500.8 1.8 fusion.139
  502.6 1.8 fusion.140
  510.2 1.8 fusion.138
  512.0 1.8 fusion.139
  513.8 1.8 fusion.140
  521.4 1.8 fusion.138
  523.2 1.8 fusion.139
  525.0 1.8 fusion.140
  532.6 1.8 fusion.138
  534.4 1.8 fusion.139
  536.2 1.8 fusion.140
  543.9 1.8 fusion.138
  545.7 1.8 fusion.139
  547.5 1.8 fusion.140
  555.1 1.8 fusion.138
  556.9 1.8 fusion.139
  566.3 1.8 fusion.138
  568.1 1.8 fusion.139
  577.5 1.8 fusion.138
  579.3 1.8 fusion.139
  588.7 1.8 fusion.138
  590.5 1.8 fusion.139
  599.9 1.8 fusion.138
  601.7 1.8 fusion.139
  611.1 1.8 fusion.138
  612.9 1.8 fusion.139
  622.3 1.8 fusion.138
  624.1 1.8 fusion.139
  633.5 1.8 fusion.138
  635.3 1.8 fusion.139
  644.7 1.8 fusion.138
  646.5 1.8 fusion.139
  655.9 1.8 fusion.138
  657.7 1.8 fusion.139
  667.0 1.8 fusion.138
  668.8 1.8 fusion.139
  672.3 7.2 convolution_convert_fusion.2
  679.6 9.7 convolution_convert_fusion.1
  689.6 11.4 %convolution_convert_fusion = bf16[4608,1152]{1,0:T(8,128)(2,1)} fusion(bf16[1,256,1152]{2,1,0:T(8,128)(2,1)} %param.31, f32[1152]{0:T(1024)S(1)} %get-tuple-element.291, f32[256,4608]{1,0:T(8,128)} %convolution_add_fusion.1), kind=kOutput, calls=%fused_computation.46 | convolution fusion | flops 2734718976 | bytes 15929856 | tf_op jit(solution)/shard_map/rsf,rsd->fd/dot_general | solution.py:202
  706.1 62.0 %all-reduce.11 = (bf16[1152]{0:T(1024)(128)(2,1)S(1)}, bf16[2304]{0:T(1024)(128)(2,1)S(1)}, bf16[1152]{0:T(1024)(128)(2,1)S(1)}, bf16[4608]{0:T(1024)(128)(2,1)S(1)}, bf16[1152]{0:T(1024)(128)(2,1)S(1)}) all-reduce(bf16[1152]{0:T(1024)(128)(2,1)S(1)} %dynamic-update-slice.3, ...), channel_id=1, replica_groups=mesh['fsdp'=16,'dp'=2] {'fsdp'}, use_global_device_ids=true, to_apply=%add.3 | all-reduce | flops 10368 | bytes 41472
  768.4 5.1 all-reduce.13
  775.7 6.8 fusion.56
  783.8 10.3 fusion.59
  794.1 109.2 %reduce-scatter.9.cloned.1.call-done = bf16[72,4608]{1,0:T(8,128)(2,1)} async-done(((bf16[1152,4608]{1,0:T(8,128)(2,1)}), bf16[72,4608]{1,0:T(8,128)(2,1)}) %reduce-scatter.9.cloned.1.call-update) | async-done | bytes 663568 | tf_op jit(solution)/shard_map/reduce_scatter | solution.py:260
  903.3 124.4 %reduce-scatter.11.cloned.1.call-done = bf16[288,1152]{1,0:T(8,128)(2,1)} async-done(((bf16[4608,1152]{1,0:T(8,128)(2,1)}), bf16[288,1152]{1,0:T(8,128)(2,1)}) %reduce-scatter.11.cloned.1.call-update) | async-done | bytes 663568 | tf_op jit(solution)/shard_map/reduce_scatter | solution.py:201
  1027.7 73.0 %all-gather.1 = bf16[32,1,6912]{2,1,0:T(2,128)(2,1)S(1)} all-gather(bf16[1,1,6912]{2,1,0:T(2,128)(2,1)S(1)} %bitcast.158), channel_id=1, replica_groups=mesh['fsdp'=16,'dp'=2] {'fsdp','dp'}, dimensions={0}, use_global_device_ids=true | all-gather | bytes 456192 | tf_op jit(solution)/shard_map/all_gather | solution.py:250
  1104.5 2.1 convert_element_type.204
  (324 shorter events, 121.0 us)
Async XLA Ops:
  7.2 72.2 %copy-start = (bf16[72,6912]{1,0:T(8,128)(2,1)S(1)}, bf16[72,6912]{1,0:T(8,128)(2,1)}, u32[]{:S(2)}) copy-start(bf16[72,6912]{1,0:T(8,128)(2,1)} %param.21) | copy-start | bytes 2985988
  7.2 160.8 %all-reduce.18.cloned.1.call-start = ((), (), s32[]{:S(2)}) async-start(), calls=%async_computation.10 | async-start | bytes 884736
  81.4 2.8 copy-start.17
  81.4 5.3 copy-start.20
  81.4 5.6 copy-start.21
  81.4 5.8 copy-start.18
  81.4 63.9 %copy-start.2 = (bf16[1,256,1152]{2,1,0:T(8,128)(2,1)S(1)}, bf16[1,256,1152]{2,1,0:T(8,128)(2,1)}, u32[]{:S(2)}) copy-start(bf16[1,256,1152]{2,1,0:T(8,128)(2,1)} %param.18) | copy-start | bytes 1769476
  81.5 160.7 %all-gather.7.cloned.1.call-start = ((), (), s32[]{:S(2)}) async-start(), calls=%async_computation.4 | async-start | bytes 8460288 | tf_op jit(solution)/shard_map/all_gather | solution.py:155
  82.2 204.2 %all-gather.9.cloned.1.call-start = ((), (), s32[]{:S(2)}) async-start(), calls=%async_computation.5 | async-start | bytes 2820096 | tf_op jit(solution)/shard_map/all_gather | solution.py:157
  82.9 292.8 %all-gather.11.cloned.1.call-start = ((), (), s32[]{:S(2)}) async-start(), calls=%async_computation.6 | async-start | bytes 11280384 | tf_op jit(solution)/shard_map/all_gather | solution.py:179
  83.5 380.9 %all-gather.13.cloned.1.call-start = ((), (), s32[]{:S(2)}) async-start(), calls=%async_computation.7 | async-start | bytes 11280384 | tf_op jit(solution)/shard_map/all_gather | solution.py:181
  84.1 709.9 %reduce-scatter.15.cloned.1.call-start = ((), (), s32[]{:S(2)}) async-start(), calls=%async_computation.12 | async-start | bytes 2820096
  242.1 6.1 copy-start.19
  280.2 6.1 copy-start.15
  280.3 10.0 copy-start.3
  375.7 88.7 %copy-start.9 = (bf16[1,256,1152]{2,1,0:T(8,128)(2,1)S(1)}, bf16[1,256,1152]{2,1,0:T(8,128)(2,1)}, u32[]{:S(2)}) copy-start(bf16[1,256,1152]{2,1,0:T(8,128)(2,1)} %param.31) | copy-start | bytes 1769476
  473.0 8.3 copy-start.12
  473.0 8.5 copy-start.10
  481.3 1.3 copy-start.5
  483.1 1.1 copy-start.4
  483.3 0.8 copy-start.8
  486.7 307.4 %reduce-scatter.13.cloned.1.call-start = ((), (), s32[]{:S(2)}) async-start(), calls=%async_computation.11 | async-start | bytes 8460288
  679.6 223.7 %reduce-scatter.9.cloned.1.call-start = ((), (), s32[]{:S(2)}) async-start(), calls=%async_computation.8 | async-start | bytes 11280384 | tf_op jit(solution)/shard_map/reduce_scatter | solution.py:260
  689.3 338.3 %reduce-scatter.11.cloned.1.call-start = ((), (), s32[]{:S(2)}) async-start(), calls=%async_computation.9 | async-start | bytes 11280384 | tf_op jit(solution)/shard_map/reduce_scatter | solution.py:201
  701.0 2.0 copy-start.22
  701.0 403.5 %all-reduce.20.cloned.1.call-start = ((), (), s32[]{:S(2)}) async-start(), calls=%async_computation.13 | async-start | bytes 3981312 | tf_op jit(solution)/shard_map/psum | solution.py:289
  775.7 8.1 copy-start.11
  782.5 1.0 copy-start.6
  1100.7 2.5 copy-start.7
  1104.5 2.1 copy-start.16
  1104.5 2.9 copy-start.14
  1106.6 1.9 copy-start.13
  1107.4 2.3 copy-start.1
Sparse Core Ops, SparseCore 0:
  81.6 86.3 all-reduce.17
  170.1 71.9 all-gather.6
  244.3 42.0 all-gather.8
  288.5 87.1 all-gather.10
  377.9 86.5 all-gather.12
  486.8 61.2 reduce-scatter.14
  679.7 99.0 reduce-scatter.12
  782.9 120.3 reduce-scatter.8
  907.3 120.2 reduce-scatter.10
  1030.0 72.9 all-reduce.19
where the time goes:
time: 1130 us; the launch traced here: 1120 us
  waiting for transfers between devices  502 us (44%)
  blocking collectives  268 us (24%)
  matrix products  226 us (20%)
  loops' own time  53.6 us (5%)
  local copies, waits for them, and re-layouts  29 us (3%)
  other arithmetic  19.3 us (2%)
  between operations  18.7 us (2%)
    reduce_scatter x1, waiting for transfers between devices, on_device(): lax.psum_scatter(jnp.einsum('rsf,rsd->fd', active, d_branch_two, preferre...  124 us
    unnamed x2, blocking collectives  120 us
    reduce_scatter x1, waiting for transfers between devices, owners(): lax.psum_scatter(term.astype(jnp.bfloat16), 'fsdp', scatter_dimension=0,...  109 us
    all_gather x1, waiting for transfers between devices, on_device(): lax.all_gather(fc1_weight, 'fsdp', axis=0, tiled=True)  85.2 us
    all_gather x1, waiting for transfers between devices, on_device(): lax.all_gather(fc2_weight, 'fsdp', axis=0, tiled=True)  79.7 us
    all_gather x1, blocking collectives, on_device(): d_mod_all = lax.all_gather(d_modulation, ('fsdp', 'dp'), axis=0, tiled=True)  73 us
    all_gather x1, waiting for transfers between devices, on_device(): lax.all_gather(qkv_weight, 'fsdp', axis=0, tiled=True)  72.5 us
    all_gather x1, blocking collectives, on_device(): act_all = lax.all_gather(cond_act, ('fsdp', 'dp'), axis=0, tiled=True)  70.5 us
  transfers between devices with their start and end apart: 10, of which 7 were waited for; matrix products, arithmetic and copies ran while one was open for 22% of the time, Pallas kernels for 0%

commit v1 on v0

--- a/solution.py
+++ b/solution.py
@@ -8,6 +8,24 @@
 root_half = 0.7978845608028654
 norm_eps = 1e-06
 masked_score = -1e30
+
+
+def gather_around(array, axis, dim):
+    ways, here, step = (lax.axis_size(axis), lax.axis_index(axis), array.shape[dim])
+    shape = [n * ways if d == dim else n for d, n in enumerate(array.shape)]
+    full = lax.dynamic_update_slice_in_dim(
+        jnp.zeros(shape, array.dtype), array, here * step, axis=dim
+    )
+    going_up = going_down = array
+    for far in range(1, ways // 2 + 1):
+        going_up = lax.ppermute(going_up, axis, [(d, (d + 1) % ways) for d in range(ways)])
+        full = lax.dynamic_update_slice_in_dim(full, going_up, (here - far) % ways * step, axis=dim)
+        if 2 * far < ways:
+            going_down = lax.ppermute(going_down, axis, [(d, (d - 1) % ways) for d in range(ways)])
+            full = lax.dynamic_update_slice_in_dim(
+                full, going_down, (here + far) % ways * step, axis=dim
+            )
+    return full
 
 
 def gelu_tanh(stream):
@@ -152,7 +170,7 @@
     ]
     shift_one, scale_one, gate_one, shift_two, scale_two, gate_two = pieces
     qkv_full, qv_bias_full, proj_full, proj_bias_full = (
-        lax.all_gather(qkv_weight, "fsdp", axis=0, tiled=True),
+        gather_around(qkv_weight, "fsdp", 0),
         lax.all_gather(qv_bias, "fsdp", axis=0, tiled=True),
         lax.all_gather(proj_weight, "fsdp", axis=0, tiled=True),
         lax.all_gather(proj_bias, "fsdp", axis=0, tiled=True),

time: 1130 us -> 1080 us (0.956)
  waiting for transfers between devices: 502 us -> 380 us
  starting transfers between devices: 0.57 us -> 53.2 us
  local copies, waits for them, and re-layouts: 29 us -> 48.2 us
    all_gather x1, waiting for transfers between devices: 85.2 us -> 4.96 us  [on_device(): lax.all_gather(fc1_weight, 'fsdp', axis=0, tiled=True)]
    all_gather x1, waiting for transfers between devices: 72.5 us -> 0.01 us  [on_device(): lax.all_gather(qkv_weight, 'fsdp', axis=0, tiled=True)]
    ppermute x0 -> x15, starting transfers between devices: none -> 52.5 us  [the longest x8 31.9 us: gather_around(): lax.ppermute(going_up, axis, [(d, (d + 1) % ways) for d in range(ways)])]
    ppermute x0 -> x15, waiting for transfers between devices: none -> 48.7 us  [the longest x8 47.7 us: gather_around(): lax.ppermute(going_up, axis, [(d, (d + 1) % ways) for d in range(ways)])]
    dynamic_update_slice x0 -> x16, local copies, waits for them, and re-layouts: none -> 14.4 us  [the longest x8 6.69 us: gather_around(): lax.dynamic_update_slice_in_dim(full, going_up, (here - far) % ways * ste...]
  transfers between devices with their start and end apart: 10 -> 25, of which waited for: 7 -> 13; matrix products, arithmetic and copies ran while one was open for 22% -> 26% of each run, Pallas kernels for 0% -> 0%
where the time goes in v1:
time: 1080 us; the launch traced here: 1070 us
  waiting for transfers between devices  380 us (35%)
  blocking collectives  270 us (25%)
  matrix products  225 us (21%)
  loops' own time  53.7 us (5%)
  starting transfers between devices  53.2 us (5%)
  local copies, waits for them, and re-layouts  48.2 us (4%)
  other arithmetic  20.3 us (2%)
  between operations  19.1 us (2%)
    reduce_scatter x1, waiting for transfers between devices, on_device(): lax.psum_scatter(jnp.einsum('rsf,rsd->fd', active, d_branch_two, preferre...  124 us
    unnamed x2, blocking collectives  122 us
    reduce_scatter x1, waiting for transfers between devices, owners(): lax.psum_scatter(term.astype(jnp.bfloat16), 'fsdp', scatter_dimension=0,...  109 us
    all_gather x1, waiting for transfers between devices, on_device(): lax.all_gather(fc2_weight, 'fsdp', axis=0, tiled=True)  78.8 us
    all_gather x1, blocking collectives, on_device(): d_mod_all = lax.all_gather(d_modulation, ('fsdp', 'dp'), axis=0, tiled=True)  73.1 us
    all_gather x1, blocking collectives, on_device(): act_all = lax.all_gather(cond_act, ('fsdp', 'dp'), axis=0, tiled=True)  70.5 us
    ppermute x8, waiting for transfers between devices, gather_around(): lax.ppermute(going_up, axis, [(d, (d + 1) % ways) for d in range(ways)])  47.7 us
    another operation x1, loops' own time, attend_back(): d_query, d_key, d_value = lax.map(one_head, jnp.arange(HEADS))  42.4 us
  transfers between devices with their start and end apart: 25, of which 13 were waited for; matrix products, arithmetic and copies ran while one was open for 26% of the time, Pallas kernels for 0%

profile of v1, /device:TPU:0, one launch (start us, length us, event | category | flops | bytes accessed | tf_op | source)
XLA Modules:
  0.0 1070.2 jit_solution(76151871287462516)
XLA Ops:
  8.0 70.5 %all-gather = bf16[32,1,1152]{2,1,0:T(2,128)(2,1)S(1)} all-gather(bf16[1,1,1152]{2,1,0:T(2,128)(2,1)S(1)} %convert_bitcast_fusion), channel_id=1, replica_groups=mesh['fsdp'=16,'dp'=2] {'fsdp','dp'}, dimensions={0}, use_global_device_ids=true | all-gather | bytes 76032 | tf_op jit(solution)/shard_map/all_gather | solution.py:153
  83.7 4.4 collective-permute-start.1
  91.5 59.3 %all-reduce.12 = (bf16[2304]{0:T(1024)(128)(2,1)S(1)}, bf16[1152]{0:T(1024)(128)(2,1)S(1)}, bf16[4608]{0:T(1024)(128)(2,1)S(1)}) all-reduce(bf16[2304]{0:T(1024)(128)(2,1)S(1)} %dynamic-update-slice, bf16[1152]{0:T(1024)(128)(2,1)S(1)} %dynamic-update-slice.1, ...), channel_id=1, replica_groups=mesh['fsdp'=16,'dp'=2] {'fsdp'}, use_global_device_ids=true, to_apply=%add | all-reduce | flops 8064 | bytes 32256
  151.7 3.7 broadcast_in_dim.88
  155.4 1.9 constant_dynamic-update-slice_fusion.21
  157.3 11.9 %all-reduce.18.cloned.1.call-done = f32[16,6912]{1,0:T(8,128)} async-done(((f32[16,6912]{1,0:T(8,128)}), f32[16,6912]{1,0:T(8,128)}) %all-reduce.18.cloned.1.call-update) | async-done | bytes 442384
  171.2 4.1 collective-permute-start.3
  176.9 5.0 collective-permute-done.2
  183.5 4.6 collective-permute-start.5
  189.8 6.8 collective-permute-done.4
  196.6 4.4 collective-permute-start.7
  202.7 5.9 collective-permute-done.6
  208.6 8.7 collective-permute-start.8
  219.9 11.0 %collective-permute-start.10 = (bf16[72,3456]{1,0:T(8,128)(2,1)S(1)}, bf16[72,3456]{1,0:T(8,128)(2,1)S(1)}, u32[]{:S(2)}, u32[]{:S(2)}) collective-permute-start(bf16[72,3456]{1,0:T(8,128)(2,1)S(1)} %collective-permute-done.8), channel_id=1, source_target_pairs={{0,2},{2,4},{4,6},{6,8},{8,10},{10,12},{12,14},{14,16},{16,18},{18... | collective-permute-start | bytes 1493000 | tf_op jit(solution)/shard_map/ppermute | solution.py:21
  232.6 4.0 collective-permute-done.10
  236.7 10.9 %collective-permute-start.12 = (bf16[72,3456]{1,0:T(8,128)(2,1)S(1)}, bf16[72,3456]{1,0:T(8,128)(2,1)S(1)}, u32[]{:S(2)}, u32[]{:S(2)}) collective-permute-start(bf16[72,3456]{1,0:T(8,128)(2,1)S(1)} %collective-permute-done.10), channel_id=1, source_target_pairs={{0,2},{2,4},{4,6},{6,8},{8,10},{10,12},{12,14},{14,16},{16,18},{18... | collective-permute-start | bytes 1493000 | tf_op jit(solution)/shard_map/ppermute | solution.py:21
  247.5 2.9 collective-permute-start.13
  252.0 15.7 %collective-permute-done.12 = bf16[72,3456]{1,0:T(8,128)(2,1)S(1)} collective-permute-done((bf16[72,3456]{1,0:T(8,128)(2,1)S(1)}, bf16[72,3456]{1,0:T(8,128)(2,1)S(1)}, u32[]{:S(2)}, u32[]{:S(2)}) %collective-permute-start.12) | collective-permute-done | bytes 497696 | tf_op jit(solution)/shard_map/ppermute | solution.py:21
  269.9 9.3 collective-permute-done.14
  280.1 6.0 fusion.37
  286.1 32.0 %while.50 = (s32[]{:T(128)}, bf16[16,256,72]{1,2,0:T(8,128)(2,1)S(1)}, f32[16,256]{1,0:T(8,128)S(1)}, s32[16]{0:T(128)S(1)}, bf16[256,3456]{1,0:T(8,128)(2,1)S(1...) while((s32[]{:T(128)}, ...), condition=%wide.region_6.7_spmd.clone, body=%wide.region_3.6_spmd.clone.sunk | while | flops 19463948 | bytes 1069367 | solution.py:89
  319.4 3.9 fusion.89
  323.5 5.0 all-gather.9.cloned.1.call-done
  328.5 9.1 convolution_add_fusion.1
  337.6 78.8 %all-gather.11.cloned.1.call-done = bf16[4608,1152]{1,0:T(8,128)(2,1)} async-done(((bf16[288,1152]{1,0:T(8,128)(2,1)}), bf16[4608,1152]{1,0:T(8,128)(2,1)}) %all-gather.11.cloned.1.call-update) | async-done | bytes 10616848 | tf_op jit(solution)/shard_map/all_gather | solution.py:199
  416.4 8.1 fusion.93
  424.5 8.3 fusion.60
  435.7 2.5 convolution_convert_fusion.3
  438.4 3.8 convolution_convert_fusion.4
  444.8 179.4 %while.51 = (s32[]{:T(128)}, bf16[16,256,72]{1,2,0:T(8,128)(2,1)}, bf16[16,256,72]{1,2,0:T(8,128)(2,1)}, bf16[16,256,72]{1,2,0:T(8,128)(2,1)}, s32[16]{0:T(128)S...) while((s32[]{:T(128)}, bf16[16,256,72]{1,2,0:T(8,128)(2,1)}, ...), condition=%wide.region_13.14_spmd.clone, body=%wide.region_11.13_spmd.clone.sunk | while | flops 47877904 | bytes 2653598 | solution.py:120
  450.8 1.8 fusion.138
  452.6 1.8 fusion.139
  462.0 1.8 fusion.138
  463.8 1.8 fusion.139
  473.2 1.8 fusion.138
  484.4 1.8 fusion.138
  495.6 1.8 fusion.138
  497.4 1.8 fusion.139
  499.2 1.8 fusion.140
  506.9 1.8 fusion.138
  518.1 1.8 fusion.138
  529.3 1.8 fusion.138
  531.1 1.8 fusion.139
  532.9 1.8 fusion.140
  540.5 1.8 fusion.138
  551.8 1.8 fusion.138
  553.6 1.8 fusion.139
  563.0 1.8 fusion.138
  574.2 1.8 fusion.138
  585.4 1.8 fusion.138
  596.6 1.8 fusion.138
  607.8 1.8 fusion.138
  618.9 1.8 fusion.138
  624.2 7.2 convolution_convert_fusion.2
  631.5 9.6 convolution_convert_fusion.1
  641.2 11.4 %convolution_convert_fusion = bf16[4608,1152]{1,0:T(8,128)(2,1)} fusion(bf16[1,256,1152]{2,1,0:T(8,128)(2,1)} %param.31, f32[1152]{0:T(1024)S(1)} %get-tuple-element.291, f32[256,4608]{1,0:T(8,128)} %convolution_add_fusion.1), kind=kOutput, calls=%fused_computation.46 | convolution fusion | flops 2734718976 | bytes 15929856 | tf_op jit(solution)/shard_map/rsf,rsd->fd/dot_general | solution.py:220
  658.0 62.3 %all-reduce.11 = (bf16[1152]{0:T(1024)(128)(2,1)S(1)}, bf16[2304]{0:T(1024)(128)(2,1)S(1)}, bf16[1152]{0:T(1024)(128)(2,1)S(1)}, bf16[4608]{0:T(1024)(128)(2,1)S(1)}, bf16[1152]{0:T(1024)(128)(2,1)S(1)}) all-reduce(bf16[1152]{0:T(1024)(128)(2,1)S(1)} %dynamic-update-slice.3, ...), channel_id=1, replica_groups=mesh['fsdp'=16,'dp'=2] {'fsdp'}, use_global_device_ids=true, to_apply=%add.3 | all-reduce | flops 10368 | bytes 41472
  720.6 4.9 all-reduce.13
  727.7 6.8 fusion.56
  735.8 10.3 fusion.59
  746.1 109.4 %reduce-scatter.9.cloned.1.call-done = bf16[72,4608]{1,0:T(8,128)(2,1)} async-done(((bf16[1152,4608]{1,0:T(8,128)(2,1)}), bf16[72,4608]{1,0:T(8,128)(2,1)}) %reduce-scatter.9.cloned.1.call-update) | async-done | bytes 663568 | tf_op jit(solution)/shard_map/reduce_scatter | solution.py:278
  855.5 124.4 %reduce-scatter.11.cloned.1.call-done = bf16[288,1152]{1,0:T(8,128)(2,1)} async-done(((bf16[4608,1152]{1,0:T(8,128)(2,1)}), bf16[288,1152]{1,0:T(8,128)(2,1)}) %reduce-scatter.11.cloned.1.call-update) | async-done | bytes 663568 | tf_op jit(solution)/shard_map/reduce_scatter | solution.py:219
  980.0 73.1 %all-gather.1 = bf16[32,1,6912]{2,1,0:T(2,128)(2,1)S(1)} all-gather(bf16[1,1,6912]{2,1,0:T(2,128)(2,1)S(1)} %bitcast.158), channel_id=1, replica_groups=mesh['fsdp'=16,'dp'=2] {'fsdp','dp'}, dimensions={0}, use_global_device_ids=true | all-gather | bytes 456192 | tf_op jit(solution)/shard_map/all_gather | solution.py:268
  1057.0 2.1 convert_element_type.204
  (369 shorter events, 163.9 us)
Async XLA Ops:
  7.2 72.2 %copy-start = (bf16[72,6912]{1,0:T(8,128)(2,1)S(1)}, bf16[72,6912]{1,0:T(8,128)(2,1)}, u32[]{:S(2)}) copy-start(bf16[72,6912]{1,0:T(8,128)(2,1)} %param.21) | copy-start | bytes 2985988
  7.2 162.0 %all-reduce.18.cloned.1.call-start = ((), (), s32[]{:S(2)}) async-start(), calls=%async_computation.10 | async-start | bytes 884736
  80.6 7.6 copy-start.16
  80.6 10.1 copy-start.19
  80.6 10.4 copy-start.20
  80.7 10.6 copy-start.17
  80.7 70.2 %copy-start.2 = (bf16[1,256,1152]{2,1,0:T(8,128)(2,1)S(1)}, bf16[1,256,1152]{2,1,0:T(8,128)(2,1)}, u32[]{:S(2)}) copy-start(bf16[1,256,1152]{2,1,0:T(8,128)(2,1)} %param.18) | copy-start | bytes 1769476
  81.5 236.7 %all-gather.7.cloned.1.call-start = ((), (), s32[]{:S(2)}) async-start(), calls=%async_computation.4 | async-start | bytes 2820096 | tf_op jit(solution)/shard_map/all_gather | solution.py:175
  82.2 246.2 %all-gather.9.cloned.1.call-start = ((), (), s32[]{:S(2)}) async-start(), calls=%async_computation.5 | async-start | bytes 11280384 | tf_op jit(solution)/shard_map/all_gather | solution.py:197
  83.0 333.4 %all-gather.11.cloned.1.call-start = ((), (), s32[]{:S(2)}) async-start(), calls=%async_computation.6 | async-start | bytes 11280384 | tf_op jit(solution)/shard_map/all_gather | solution.py:199
  83.6 644.2 %all-gather.13.cloned.1.call-start = ((), (), s32[]{:S(2)}) async-start(), calls=%async_computation.7 | async-start | bytes 8460288 | tf_op jit(solution)/shard_map/all_gather | solution.py:236
  83.6 87.2 %collective-permute-start = (bf16[72,3456]{1,0:T(8,128)(2,1)}, bf16[72,3456]{1,0:T(8,128)(2,1)S(1)}, u32[]{:S(2)}, u32[]{:S(2)}) collective-permute-start(bf16[72,3456]{1,0:T(8,128)(2,1)} %param.23), channel_id=1, source_target_pairs={{0,2},{2,4},{4,6},{6,8},{8,10},{10,12},{12,14},{14,16},{16,18},{18... | collective-permute-start | bytes 1493000 | tf_op jit(solution)/shard_map/ppermute | solution.py:21
  83.7 87.6 %collective-permute-start.1 = (bf16[72,3456]{1,0:T(8,128)(2,1)}, bf16[72,3456]{1,0:T(8,128)(2,1)S(1)}, u32[]{:S(2)}, u32[]{:S(2)}) collective-permute-start(bf16[72,3456]{1,0:T(8,128)(2,1)} %param.23), channel_id=1, source_target_pairs={{0,30},{2,0},{4,2},{6,4},{8,6},{10,8},{12,10},{14,12},{16,14},{18,... | collective-permute-start | bytes 1493000 | tf_op jit(solution)/shard_map/ppermute | solution.py:24
  88.1 658.0 %reduce-scatter.15.cloned.1.call-start = ((), (), s32[]{:S(2)}) async-start(), calls=%async_computation.12 | async-start | bytes 2820096
  170.8 11.2 %collective-permute-start.2 = (bf16[72,3456]{1,0:T(8,128)(2,1)S(1)}, bf16[72,3456]{1,0:T(8,128)(2,1)S(1)}, u32[]{:S(2)}, u32[]{:S(2)}) collective-permute-start(bf16[72,3456]{1,0:T(8,128)(2,1)S(1)} %collective-permute-done), channel_id=1, source_target_pairs={{0,2},{2,4},{4,6},{6,8},{8,10},{10,12},{12,14},{14,16},{16,18},{18... | collective-permute-start | bytes 1493000 | tf_op jit(solution)/shard_map/ppermute | solution.py:21
  171.2 12.3 %collective-permute-start.3 = (bf16[72,3456]{1,0:T(8,128)(2,1)S(1)}, bf16[72,3456]{1,0:T(8,128)(2,1)S(1)}, u32[]{:S(2)}, u32[]{:S(2)}) collective-permute-start(bf16[72,3456]{1,0:T(8,128)(2,1)S(1)} %collective-permute-done.1), channel_id=1, source_target_pairs={{0,30},{2,0},{4,2},{6,4},{8,6},{10,8},{12,10},{14,12},{16,14},{18,... | collective-permute-start | bytes 1493000 | tf_op jit(solution)/shard_map/ppermute | solution.py:24
  182.0 14.6 %collective-permute-start.4 = (bf16[72,3456]{1,0:T(8,128)(2,1)S(1)}, bf16[72,3456]{1,0:T(8,128)(2,1)S(1)}, u32[]{:S(2)}, u32[]{:S(2)}) collective-permute-start(bf16[72,3456]{1,0:T(8,128)(2,1)S(1)} %collective-permute-done.2), channel_id=1, source_target_pairs={{0,2},{2,4},{4,6},{6,8},{8,10},{10,12},{12,14},{14,16},{16,18},{18... | collective-permute-start | bytes 1493000 | tf_op jit(solution)/shard_map/ppermute | solution.py:21
  183.5 13.1 %collective-permute-start.5 = (bf16[72,3456]{1,0:T(8,128)(2,1)S(1)}, bf16[72,3456]{1,0:T(8,128)(2,1)S(1)}, u32[]{:S(2)}, u32[]{:S(2)}) collective-permute-start(bf16[72,3456]{1,0:T(8,128)(2,1)S(1)} %collective-permute-done.3), channel_id=1, source_target_pairs={{0,30},{2,0},{4,2},{6,4},{8,6},{10,8},{12,10},{14,12},{16,14},{18,... | collective-permute-start | bytes 1493000 | tf_op jit(solution)/shard_map/ppermute | solution.py:24
  196.6 12.0 %collective-permute-start.6 = (bf16[72,3456]{1,0:T(8,128)(2,1)S(1)}, bf16[72,3456]{1,0:T(8,128)(2,1)S(1)}, u32[]{:S(2)}, u32[]{:S(2)}) collective-permute-start(bf16[72,3456]{1,0:T(8,128)(2,1)S(1)} %collective-permute-done.4), channel_id=1, source_target_pairs={{0,2},{2,4},{4,6},{6,8},{8,10},{10,12},{12,14},{14,16},{16,18},{18... | collective-permute-start | bytes 1493000 | tf_op jit(solution)/shard_map/ppermute | solution.py:21
  196.6 20.7 %collective-permute-start.7 = (bf16[72,3456]{1,0:T(8,128)(2,1)S(1)}, bf16[72,3456]{1,0:T(8,128)(2,1)S(1)}, u32[]{:S(2)}, u32[]{:S(2)}) collective-permute-start(bf16[72,3456]{1,0:T(8,128)(2,1)S(1)} %collective-permute-done.5), channel_id=1, source_target_pairs={{0,30},{2,0},{4,2},{6,4},{8,6},{10,8},{12,10},{14,12},{16,14},{18,... | collective-permute-start | bytes 1493000 | tf_op jit(solution)/shard_map/ppermute | solution.py:24
  208.6 11.3 %collective-permute-start.8 = (bf16[72,3456]{1,0:T(8,128)(2,1)S(1)}, bf16[72,3456]{1,0:T(8,128)(2,1)S(1)}, u32[]{:S(2)}, u32[]{:S(2)}) collective-permute-start(bf16[72,3456]{1,0:T(8,128)(2,1)S(1)} %collective-permute-done.6), channel_id=1, source_target_pairs={{0,2},{2,4},{4,6},{6,8},{8,10},{10,12},{12,14},{14,16},{16,18},{18... | collective-permute-start | bytes 1493000 | tf_op jit(solution)/shard_map/ppermute | solution.py:21
  217.3 13.7 %collective-permute-start.9 = (bf16[72,3456]{1,0:T(8,128)(2,1)S(1)}, bf16[72,3456]{1,0:T(8,128)(2,1)S(1)}, u32[]{:S(2)}, u32[]{:S(2)}) collective-permute-start(bf16[72,3456]{1,0:T(8,128)(2,1)S(1)} %collective-permute-done.7), channel_id=1, source_target_pairs={{0,30},{2,0},{4,2},{6,4},{8,6},{10,8},{12,10},{14,12},{16,14},{18,... | collective-permute-start | bytes 1493000 | tf_op jit(solution)/shard_map/ppermute | solution.py:24
  219.9 16.7 %collective-permute-start.10 = (bf16[72,3456]{1,0:T(8,128)(2,1)S(1)}, bf16[72,3456]{1,0:T(8,128)(2,1)S(1)}, u32[]{:S(2)}, u32[]{:S(2)}) collective-permute-start(bf16[72,3456]{1,0:T(8,128)(2,1)S(1)} %collective-permute-done.8), channel_id=1, source_target_pairs={{0,2},{2,4},{4,6},{6,8},{8,10},{10,12},{12,14},{14,16},{16,18},{18... | collective-permute-start | bytes 1493000 | tf_op jit(solution)/shard_map/ppermute | solution.py:21
  231.0 16.6 %collective-permute-start.11 = (bf16[72,3456]{1,0:T(8,128)(2,1)S(1)}, bf16[72,3456]{1,0:T(8,128)(2,1)S(1)}, u32[]{:S(2)}, u32[]{:S(2)}) collective-permute-start(bf16[72,3456]{1,0:T(8,128)(2,1)S(1)} %collective-permute-done.9), channel_id=1, source_target_pairs={{0,30},{2,0},{4,2},{6,4},{8,6},{10,8},{12,10},{14,12},{16,14},{18,... | collective-permute-start | bytes 1493000 | tf_op jit(solution)/shard_map/ppermute | solution.py:24
  236.7 31.1 %collective-permute-start.12 = (bf16[72,3456]{1,0:T(8,128)(2,1)S(1)}, bf16[72,3456]{1,0:T(8,128)(2,1)S(1)}, u32[]{:S(2)}, u32[]{:S(2)}) collective-permute-start(bf16[72,3456]{1,0:T(8,128)(2,1)S(1)} %collective-permute-done.10), channel_id=1, source_target_pairs={{0,2},{2,4},{4,6},{6,8},{8,10},{10,12},{12,14},{14,16},{16,18},{18... | collective-permute-start | bytes 1493000 | tf_op jit(solution)/shard_map/ppermute | solution.py:21
  247.5 21.6 %collective-permute-start.13 = (bf16[72,3456]{1,0:T(8,128)(2,1)S(1)}, bf16[72,3456]{1,0:T(8,128)(2,1)S(1)}, u32[]{:S(2)}, u32[]{:S(2)}) collective-permute-start(bf16[72,3456]{1,0:T(8,128)(2,1)S(1)} %collective-permute-done.11), channel_id=1, source_target_pairs={{0,30},{2,0},{4,2},{6,4},{8,6},{10,8},{12,10},{14,12},{16,14},{18,... | collective-permute-start | bytes 1493000 | tf_op jit(solution)/shard_map/ppermute | solution.py:24
  267.7 11.5 %collective-permute-start.14 = (bf16[72,3456]{1,0:T(8,128)(2,1)S(1)}, bf16[72,3456]{1,0:T(8,128)(2,1)S(1)}, u32[]{:S(2)}, u32[]{:S(2)}) collective-permute-start(bf16[72,3456]{1,0:T(8,128)(2,1)S(1)} %collective-permute-done.12), channel_id=1, source_target_pairs={{0,2},{2,4},{4,6},{6,8},{8,10},{10,12},{12,14},{14,16},{16,18},{18... | collective-permute-start | bytes 1493000 | tf_op jit(solution)/shard_map/ppermute | solution.py:21
  280.1 6.1 copy-start.18
  318.2 1.2 copy-start.15
  318.2 5.1 copy-start.3
  328.5 87.9 %copy-start.9 = (bf16[1,256,1152]{2,1,0:T(8,128)(2,1)S(1)}, bf16[1,256,1152]{2,1,0:T(8,128)(2,1)}, u32[]{:S(2)}) copy-start(bf16[1,256,1152]{2,1,0:T(8,128)(2,1)} %param.31) | copy-start | bytes 1769476
  424.5 8.3 copy-start.12
  424.5 8.6 copy-start.10
  432.8 1.3 copy-start.5
  434.6 1.1 copy-start.4
  434.8 0.8 copy-start.8
  438.2 307.9 %reduce-scatter.13.cloned.1.call-start = ((), (), s32[]{:S(2)}) async-start(), calls=%async_computation.11 | async-start | bytes 8460288
  631.5 224.1 %reduce-scatter.9.cloned.1.call-start = ((), (), s32[]{:S(2)}) async-start(), calls=%async_computation.8 | async-start | bytes 11280384 | tf_op jit(solution)/shard_map/reduce_scatter | solution.py:278
  641.2 338.8 %reduce-scatter.11.cloned.1.call-start = ((), (), s32[]{:S(2)}) async-start(), calls=%async_computation.9 | async-start | bytes 11280384 | tf_op jit(solution)/shard_map/reduce_scatter | solution.py:219
  652.6 2.2 copy-start.21
  652.6 404.3 %all-reduce.20.cloned.1.call-start = ((), (), s32[]{:S(2)}) async-start(), calls=%async_computation.13 | async-start | bytes 3981312 | tf_op jit(solution)/shard_map/psum | solution.py:307
  727.7 8.1 copy-start.11
  734.5 1.0 copy-start.6
  980.0 75.7 %copy-start.7 = (f32[256,1152]{1,0:T(8,128)S(1)}, f32[256,1152]{1,0:T(8,128)}, u32[]{:S(2)}) copy-start(f32[256,1152]{1,0:T(8,128)} %copy-done.6) | copy-start | bytes 3538948
  1056.9 3.8 copy-start.14
  1057.0 5.0 copy-start.13
  1060.8 2.3 copy-start.1
Sparse Core Ops, SparseCore 0:
  81.6 87.4 all-reduce.17
  171.3 58.9 all-gather.6
  232.6 95.8 all-gather.8
  330.6 85.7 all-gather.10
  418.4 69.8 all-gather.12
  492.0 61.6 reduce-scatter.14
  631.6 99.4 reduce-scatter.12
  735.1 120.3 reduce-scatter.8
  859.6 120.2 reduce-scatter.10
  982.3 72.9 all-reduce.19
